TPU v7x, 512 devices: a whole 4x8x8 slice. The times are simulated.
512 devices in a mesh: dp: 64 (over y_lo, z, core), tensor: 8 (over y_hi, x).
Axes of the slice: x: 4, y: 8 (y_hi: 2, y_lo: 4; y = y_hi * 4 + y_lo), z: 8, core: 2. Of those that a mesh axis runs over, the one named last changes fastest.
Arguments:
- hidden_rows: bfloat16 [4096, 16384], P('dp', 'tensor')
- norm_gain: float32 [16384], P('tensor'), may hold values from 0.5 to 1.5
- key_weight: bfloat16 [512, 16384], P('dp', 'tensor'), may hold values from -0.046875 to 0.046875
- cotangent: bfloat16 [64, 128, 512], P('dp'), may hold values from -16 to 16
- accepted_counts: int32 [64], P('dp'), may hold values from 16 to 64, as said below
- destination: int32 [4096], P('dp'), may hold values from 0 to 63, as said below
Outputs:
- keys: bfloat16 [64, 128, 512], P('dp')
- key_weight_grad: float32 [512, 16384], P('dp', 'tensor')
- gain_grad: float32 [16384], P('tensor')
Inputs may be any that keep to these rules, and one draw needn't show every extreme that they name: `accepted_counts`: rows 0 to the count minus 1 of a replica are accepted; in every draw one replica accepts all its rows and another a quarter of them. `destination`: among one replica's 64 rows no shard is named more than 2 times; in every draw one shard is named exactly 2 times by every replica, all within the first quarter of that replica's rows.
All inputs are finite; a program needn't handle non-finite values.
Results may differ from a plain program's by a relative error of at most 0.0051.
Values may be sent and summed in bfloat16 or wider, within the bound.
A program may use at most 64 MiB of HBM per device.

v0:
```python
import math
import jax
import jax.numpy as jnp
from jax import lax
from jax.sharding import PartitionSpec as P

D = 16384
EPSILON = 1e-05


def slot_layout(dest_rows, count, groups, capacity):
    row_total = dest_rows.shape[0]
    row_order = lax.broadcasted_iota(jnp.int32, (row_total,), 0)
    onehot = (dest_rows[:, None] == lax.broadcasted_iota(jnp.int32, (row_total, groups), 1)).astype(
        jnp.int32
    )
    before = jnp.cumsum(onehot, axis=0) - onehot
    slot_rank = jnp.sum(before * onehot, axis=1)
    accepted = row_order < count
    position = dest_rows * capacity + slot_rank
    filler = jnp.full((groups * capacity,), row_total, jnp.int32)
    filler = filler.at[jnp.where(accepted, position, groups * capacity)].set(row_order, mode="drop")
    return (accepted, position, filler)


def with_blank(source_table):
    return jnp.concatenate(
        [source_table, jnp.zeros((1, source_table.shape[1]), source_table.dtype)], axis=0
    )


def on_device(hidden_rows, norm_gain, key_weight, cotangent, accepted_counts, destination):
    replicas = lax.axis_size("dp")
    own_rows = hidden_rows.shape[0]
    capacity = 2 * own_rows // replicas
    accepted, position, filler = slot_layout(destination, accepted_counts[0], replicas, capacity)
    row_data = lax.all_to_all(
        with_blank(hidden_rows)[filler], "dp", split_axis=0, concat_axis=0, tiled=True
    )
    row_cot = cotangent[0]
    row_float = row_data.astype(jnp.float32)
    squares = lax.psum(jnp.sum(row_float * row_float, axis=1), "tensor")
    normed = (row_float * lax.rsqrt(squares / D + EPSILON)[:, None] * norm_gain[None, :]).astype(
        jnp.bfloat16
    )
    weights_whole = lax.all_gather(key_weight, "dp", axis=0, tiled=True)
    partial_value = lax.dot_general(
        normed, weights_whole, (((1,), (1,)), ((), ())), preferred_element_type=jnp.float32
    )
    backward = jnp.dot(row_cot, weights_whole, preferred_element_type=jnp.float32)
    row_keys = lax.psum(partial_value, "tensor").astype(jnp.bfloat16)
    factor = 1.0 / math.sqrt(own_rows * replicas)
    grad_weight = (
        lax.psum_scatter(
            lax.dot_general(
                row_cot, normed, (((0,), (0,)), ((), ())), preferred_element_type=jnp.float32
            ),
            "dp",
            scatter_dimension=0,
            tiled=True,
        )
        * factor
    )
    gain_term = jnp.sum(backward * normed.astype(jnp.float32), axis=0)
    grad_gain = lax.psum(gain_term, "dp") * factor / norm_gain
    return (row_keys[None], grad_weight, grad_gain)


def solution(mesh):
    return jax.shard_map(
        on_device,
        mesh=mesh,
        in_specs=(
            P("dp", "tensor"),
            P("tensor"),
            P("dp", "tensor"),
            P("dp", None, None),
            P("dp"),
            P("dp"),
        ),
        out_specs=(P("dp", None, None), P("dp", "tensor"), P("tensor")),
        check_vma=False,
    )
```

profile of v0, /device:TPU:6, one launch (start us, length us, event | category | flops | bytes accessed | tf_op | source)
XLA Modules:
  0.0 436.4 jit_solution(2184907873028048254)
XLA Ops:
  7.2 0.0 copy-start
  7.2 0.0 all-gather.2.cloned.1.call-start
  7.2 0.7 all-gather.2.cloned.1.call-update
  7.9 0.0 reduce-scatter.4.cloned.1.call-start
  8.6 0.7 fusion.3
  9.3 0.1 reduce_window_sum.11
  9.4 1.0 concatenate.3
  10.4 0.8 select_reduce_fusion
  11.3 0.7 compare_select_fusion.1
  11.9 0.8 scatter_custom_fusion
  12.7 0.9 gather_fusion
  13.7 0.0 copy-start.2
  13.7 0.3 all_to_all.6
  14.0 32.0 %all_to_all.9 = bf16[64,2,2048]{2,1,0:T(2,128)(2,1)S(1)} all-to-all(bf16[64,2,2048]{2,1,0:T(2,128)(2,1)S(1)} %all_to_all.6), channel_id=1, replica_groups=mesh['dp'=64,'tensor'=8] {'dp'}, dimensions={0} | all-to-all | bytes 1048576 | tf_op jit(solution)/shard_map/all_to_all | solution.py:37
  46.1 0.6 multiply_reduce_fusion
  46.7 0.1 reduce_sum.31
  46.8 23.5 %psum.21 = f32[128]{0:T(128)S(1)} all-reduce(f32[128]{0:T(128)S(1)} %reduce_sum.31), channel_id=1, replica_groups=mesh['dp'=64,'tensor'=8] {'tensor'}, use_global_device_ids=true, to_apply=%region_4.5 | all-reduce | flops 128 | bytes 1024 | tf_op jit(solution)/shard_map/psum | solution.py:42
  70.3 0.1 mul.64
  70.5 0.0 copy-done.2
  70.5 0.6 multiply_convert_fusion
  71.1 0.2 convert_element_type.34
  71.3 0.0 copy-done
  71.3 2.7 convolution_bitcast_fusion
  74.0 5.4 %copy.12 = f32[512,2048]{1,0:T(8,128)} copy(f32[512,2048]{0,1:T(8,128)} %convolution_bitcast_fusion) | data formatting | bytes 8388608
  79.4 0.0 reduce-scatter.4.cloned.1.call-update
  79.4 0.1 reshape.23
  79.6 58.5 %all-gather.2.cloned.1.call-done = bf16[512,2048]{1,0:T(8,128)(2,1)} async-done(((bf16[8,2048]{1,0:T(8,128)(2,1)}), bf16[512,2048]{1,0:T(8,128)(2,1)}) %all-gather.2.cloned.1.call-update) | async-done | bytes 2097168 | tf_op jit(solution)/shard_map/all_gather | solution.py:46
  138.1 0.0 copy-start.1
  138.1 2.6 fusion.6
  140.7 0.0 copy-done.1
  140.7 0.6 fusion
  141.3 137.8 %psum.23 = f32[2048]{0:T(1024)S(1)} all-reduce(f32[2048]{0:T(1024)S(1)} %fusion), channel_id=1, replica_groups=mesh['dp'=64,'tensor'=8] {'dp'}, use_global_device_ids=true, to_apply=%region_8.9 | all-reduce | flops 2048 | bytes 16384 | tf_op jit(solution)/shard_map/psum | solution.py:65
  279.1 0.6 multiply_divide_fusion
  279.7 49.9 %all-reduce.2 = bf16[128,512]{1,0:T(8,128)(2,1)} all-reduce(f32[128,512]{1,0:T(8,128)S(1)} %fusion.6), channel_id=1, replica_groups=mesh['dp'=64,'tensor'=8] {'tensor'}, use_global_device_ids=true, to_apply=%region_5.6 | all-reduce | flops 65536 | bytes 393216 | tf_op jit(solution)/shard_map/psum | solution.py:51
  329.6 97.8 %reduce-scatter.4.cloned.1.call-done = f32[8,2048]{1,0:T(8,128)} async-done(((f32[512,2048]{1,0:T(8,128)}), f32[8,2048]{1,0:T(8,128)}) %reduce-scatter.4.cloned.1.call-update) | async-done | bytes 65552
  427.4 1.2 copy.13
  428.5 0.1 broadcast_multiply_fusion
  428.6 0.9 copy.11
  (4 shorter events, 0.0 us)
Async XLA Ops:
  7.2 64.2 %copy-start = (bf16[1,128,512]{2,1,0:T(8,128)(2,1)S(1)}, bf16[1,128,512]{2,1,0:T(8,128)(2,1)}, u32[]{:S(2)}) copy-start(bf16[1,128,512]{2,1,0:T(8,128)(2,1)} %param.9) | copy-start | bytes 393220
  7.2 130.9 %all-gather.2.cloned.1.call-start = ((), (), s32[]{:S(2)}) async-start(), calls=%async_computation.2 | async-start | bytes 2129920 | tf_op jit(solution)/shard_map/all_gather | solution.py:46
  7.9 419.5 %reduce-scatter.4.cloned.1.call-start = ((), (), s32[]{:S(2)}) async-start(), calls=%async_computation.3 | async-start | bytes 4259840
  13.7 56.8 %copy-start.2 = (f32[2048]{0:T(1024)S(1)}, f32[2048]{0:T(1024)}, u32[]{:S(2)}) copy-start(f32[2048]{0:T(1024)} %param.7) | copy-start | bytes 24580
  138.1 2.6 copy-start.1
Sparse Core Ops, SparseCore 0:
  10.2 127.8 all-gather.1
  140.9 286.4 reduce-scatter.3
where the time goes:
time: 437 us; the launch traced here: 436 us
  blocking collectives  243 us (56%)
  waiting for transfers between devices  157 us (36%)
  between operations  14.8 us (3%)
  local copies, waits for them, and re-layouts  11.1 us (3%)
  matrix products  5.84 us (1%)
    psum x1, blocking collectives, on_device(): grad_gain = lax.psum(gain_term, 'dp') * factor / norm_gain  138 us
    unnamed x3, waiting for transfers between devices  98.5 us
    all_gather x1, waiting for transfers between devices, on_device(): weights_whole = lax.all_gather(key_weight, 'dp', axis=0, tiled=True)  58.5 us
    psum x1, blocking collectives, on_device(): row_keys = lax.psum(partial_value, 'tensor').astype(jnp.bfloat16)  49.9 us
    all_to_all x1, blocking collectives, on_device(): lax.all_to_all(with_blank(hidden_rows)[filler], 'dp', split_axis=0, conca...  32 us
    psum x1, blocking collectives, on_device(): squares = lax.psum(jnp.sum(row_float * row_float, axis=1), 'tensor')  23.5 us
  transfers between devices with their start and end apart: 2, of which 2 were waited for; matrix products, arithmetic and copies ran while one was open for 4% of the time, Pallas kernels for 0%

commit v1 on v0

--- a/solution.py
+++ b/solution.py
@@ -43,7 +43,9 @@
     normed = (row_float * lax.rsqrt(squares / D + EPSILON)[:, None] * norm_gain[None, :]).astype(
         jnp.bfloat16
     )
-    weights_whole = lax.all_gather(key_weight, "dp", axis=0, tiled=True)
+    weights_whole = jnp.concatenate(
+        lax.all_to_all(jnp.stack([key_weight] * lax.axis_size("dp")), "dp", 0, 0), axis=0
+    )
     partial_value = lax.dot_general(
         normed, weights_whole, (((1,), (1,)), ((), ())), preferred_element_type=jnp.float32
     )

time: 437 us -> 405 us (0.927); the launches traced: 436 us -> 399 us
  waiting for transfers between devices: 157 us -> 104 us
  blocking collectives: 243 us -> 251 us
  starting transfers between devices: 0.08 us -> 6.15 us
    all_gather x1 -> x0, waiting for transfers between devices: 58.5 us -> none  [on_device(): weights_whole = lax.all_gather(key_weight, 'dp', axis=0, tiled=True)]
    all_to_all x0 -> x1, waiting for transfers between devices: none -> 50.1 us  [on_device(): lax.all_to_all(jnp.stack([key_weight] * lax.axis_size('dp')), 'dp', 0, 0)]
    unnamed x3 -> x2, waiting for transfers between devices: 98.5 us -> 53.4 us
    psum x1, blocking collectives: 138 us -> 144 us  [on_device(): grad_gain = lax.psum(gain_term, 'dp') * factor / norm_gain]
    all_to_all x0 -> x1, starting transfers between devices: none -> 6.11 us  [on_device(): lax.all_to_all(jnp.stack([key_weight] * lax.axis_size('dp')), 'dp', 0, 0)]
  transfers between devices with their start and end apart: 2 -> 2, of which waited for: 2 -> 2; matrix products, arithmetic and copies ran while one was open for 4% -> 1% of each run, Pallas kernels for 0% -> 0%
where the time goes in v1:
time: 405 us; the launch traced here: 399 us
  blocking collectives  251 us (62%)
  waiting for transfers between devices  104 us (26%)
  between operations  14.9 us (4%)
  local copies, waits for them, and re-layouts  14.8 us (4%)
  starting transfers between devices  6.15 us (2%)
  other arithmetic  4.26 us (1%)
  matrix products  4.08 us (1%)
    psum x1, blocking collectives, on_device(): grad_gain = lax.psum(gain_term, 'dp') * factor / norm_gain  144 us
    unnamed x2, waiting for transfers between devices  53.4 us
    psum x1, blocking collectives, on_device(): row_keys = lax.psum(partial_value, 'tensor').astype(jnp.bfloat16)  52.1 us
    all_to_all x1, waiting for transfers between devices, on_device(): lax.all_to_all(jnp.stack([key_weight] * lax.axis_size('dp')), 'dp', 0, 0)  50.1 us
    all_to_all x1, blocking collectives, on_device(): lax.all_to_all(with_blank(hidden_rows)[filler], 'dp', split_axis=0, conca...  31.2 us
    psum x1, blocking collectives, on_device(): squares = lax.psum(jnp.sum(row_float * row_float, axis=1), 'tensor')  23.5 us
    unnamed x11, local copies, waits for them, and re-layouts  8.61 us
  transfers between devices with their start and end apart: 2, of which 2 were waited for; matrix products, arithmetic and copies ran while one was open for 1% of the time, Pallas kernels for 0%

profile of v1, /device:TPU:6, one launch (start us, length us, event | category | flops | bytes accessed | tf_op | source)
XLA Modules:
  0.0 398.8 jit_solution(458854444109994631)
XLA Ops:
  7.2 0.0 copy-start
  7.2 0.0 reduce-scatter.4.cloned.1.call-start
  7.9 0.7 fusion.8
  8.6 0.1 reduce_window_sum.11
  8.7 0.8 select_reduce_fusion
  9.6 0.7 compare_select_fusion.1
  10.2 0.8 scatter_custom_fusion
  11.0 1.0 concatenate.3
  12.0 0.9 gather_fusion
  13.0 0.0 copy-start.2
  13.0 0.3 all_to_all.9
  13.3 31.2 %all_to_all.14 = bf16[64,2,2048]{2,1,0:T(2,128)(2,1)S(1)} all-to-all(bf16[64,2,2048]{2,1,0:T(2,128)(2,1)S(1)} %all_to_all.9), channel_id=1, replica_groups=mesh['dp'=64,'tensor'=8] {'dp'}, dimensions={0} | all-to-all | bytes 1048576 | tf_op jit(solution)/shard_map/all_to_all | solution.py:37
  44.6 0.6 multiply_reduce_fusion
  45.2 0.1 reduce_sum.31
  45.3 23.5 %psum.21 = f32[128]{0:T(128)S(1)} all-reduce(f32[128]{0:T(128)S(1)} %reduce_sum.31), channel_id=1, replica_groups=mesh['dp'=64,'tensor'=8] {'tensor'}, use_global_device_ids=true, to_apply=%region_4.5 | all-reduce | flops 128 | bytes 1024 | tf_op jit(solution)/shard_map/psum | solution.py:42
  68.9 0.1 mul.62
  69.0 0.0 copy-done.2
  69.0 0.6 multiply_convert_fusion.1
  69.7 0.2 convert_element_type.32
  69.9 0.0 copy-done
  69.9 2.7 convolution_bitcast_fusion
  72.6 5.4 %copy.12 = f32[512,2048]{1,0:T(8,128)} copy(f32[512,2048]{0,1:T(8,128)} %convolution_bitcast_fusion) | data formatting | bytes 8388608
  77.9 0.0 copy-start.3
  77.9 0.0 reduce-scatter.4.cloned.1.call-update
  78.0 0.7 copy-done.3
  78.7 1.6 stack.2
  80.3 6.1 %all-to-all-start.1 = ((bf16[64,8,2048]{2,1,0:T(8,128)(2,1)}), bf16[64,8,2048]{2,1,0:T(8,128)(2,1)S(1)}, u32[]{:S(2)}, u32[]{:S(2)}) async-start(bf16[64,8,2048]{2,1,0:T(8,128)(2,1)} %stack.2), calls=%async_computation.1 | async-start | bytes 4194304 | tf_op jit(solution)/shard_map/all_to_all | solution.py:47
  86.4 1.2 reshape.40
  87.6 50.1 %all-to-all-done.1 = bf16[64,8,2048]{2,1,0:T(8,128)(2,1)S(1)} async-done(((bf16[64,8,2048]{2,1,0:T(8,128)(2,1)}), bf16[64,8,2048]{2,1,0:T(8,128)(2,1)S(1)}, u32[]{:S(2)}, u32[]{:S(2)}) %all-to-all-start.1) | async-done | bytes 2097184 | tf_op jit(solution)/shard_map/all_to_all | solution.py:47
  137.7 0.0 copy-start.1
  137.7 0.8 fusion.1
  138.5 0.4 copy-done.1
  138.9 0.6 fusion.3
  139.5 144.1 %psum.23 = f32[2048]{0:T(1024)S(1)} all-reduce(f32[2048]{0:T(1024)S(1)} %fusion.3), channel_id=1, replica_groups=mesh['dp'=64,'tensor'=8] {'dp'}, use_global_device_ids=true, to_apply=%region_8.9 | all-reduce | flops 2048 | bytes 16384 | tf_op jit(solution)/shard_map/psum | solution.py:67
  283.6 0.6 multiply_divide_fusion
  284.2 52.1 %all-reduce.2 = bf16[128,512]{1,0:T(8,128)(2,1)} all-reduce(f32[128,512]{1,0:T(8,128)S(1)} %fusion.1), channel_id=1, replica_groups=mesh['dp'=64,'tensor'=8] {'tensor'}, use_global_device_ids=true, to_apply=%region_5.6 | all-reduce | flops 65536 | bytes 393216 | tf_op jit(solution)/shard_map/psum | solution.py:53
  336.3 53.4 %reduce-scatter.4.cloned.1.call-done = f32[8,2048]{1,0:T(8,128)} async-done(((f32[512,2048]{1,0:T(8,128)}), f32[8,2048]{1,0:T(8,128)}) %reduce-scatter.4.cloned.1.call-update) | async-done | bytes 65552
  389.8 1.2 copy.13
  390.9 0.1 broadcast_multiply_fusion
  391.0 0.9 copy.11
  (4 shorter events, 0.0 us)
Async XLA Ops:
  7.2 62.7 %copy-start = (bf16[1,128,512]{2,1,0:T(8,128)(2,1)S(1)}, bf16[1,128,512]{2,1,0:T(8,128)(2,1)}, u32[]{:S(2)}) copy-start(bf16[1,128,512]{2,1,0:T(8,128)(2,1)} %param.9) | copy-start | bytes 393220
  7.2 382.6 %reduce-scatter.4.cloned.1.call-start = ((), (), s32[]{:S(2)}) async-start(), calls=%async_computation.3 | async-start | bytes 4259840
  13.0 56.1 %copy-start.2 = (f32[2048]{0:T(1024)S(1)}, f32[2048]{0:T(1024)}, u32[]{:S(2)}) copy-start(f32[2048]{0:T(1024)} %param.7) | copy-start | bytes 24580
  77.9 0.8 copy-start.3
  80.3 57.4 %all-to-all-start.1 = ((bf16[64,8,2048]{2,1,0:T(8,128)(2,1)}), bf16[64,8,2048]{2,1,0:T(8,128)(2,1)S(1)}, u32[]{:S(2)}, u32[]{:S(2)}) async-start(bf16[64,8,2048]{2,1,0:T(8,128)(2,1)} %stack.2), calls=%async_computation.1 | async-start | bytes 4194304 | tf_op jit(solution)/shard_map/all_to_all | solution.py:47
  137.7 1.2 copy-start.1
Sparse Core Ops, SparseCore 0:
  78.1 311.6 reduce-scatter.3
